TPU v7x, 32 devices: a whole 2x2x4 slice. The times are simulated.
32 devices in a mesh: ctx: 8 (over z, x), head: 4 (over y, core).
Axes of the slice: x: 2, y: 2, z: 4, core: 2. Of those that a mesh axis runs over, the one named last changes fastest.
Arguments:
- events: bfloat16 [2048, 512], P('ctx', 'head'), may hold values from -6 to 6
- w_proj: bfloat16 [3, 512, 128], P(None, 'head'), may hold values from -0.5091169 to 0.5091169
- targets: bfloat16 [2048, 512], P('ctx', 'head'), may hold values from -6 to 6
- negatives: bfloat16 [1920, 512], P(None, 'head'), may hold values from -6 to 6
- owners: int32 [2048, 1], P('ctx'), may hold values from 0 to 7; in each aligned block of 256 rows (0 to 255, 256 to 511, ...) at most 48 rows name the same one
- item_rows: int32 [2048], P('ctx'), may hold values from 0 to 511
Outputs:
- table_grad: float32 [4096, 512], P('ctx', 'head')
Inputs may be any that keep to these rules, and one draw needn't show every extreme that they name: `owners`: among the 256 events on one index of ctx (aligned blocks of 256 rows), no owner is named more than 48 times, a bound that some block reaches.
All inputs are finite; a program needn't handle non-finite values.
Results may differ from a plain program's by a relative error of at most 0.0055.
Values may be sent and summed in bfloat16 or wider, within the bound.
A program may use at most 64 MiB of HBM per device.

v0:
```python
import math

import jax
import jax.numpy as jnp
from jax import lax
from jax.sharding import PartitionSpec as P

ROWS_OWN = 512


highest = lax.Precision.HIGHEST


def carried_in(shard, axis, combine, identity, reverse):
    length, here = (lax.axis_size(axis), lax.axis_index(axis))
    everything = jax.tree.map(lambda part: lax.all_gather(part, axis), shard)
    start = jax.tree.map(
        lambda part, zero: jnp.broadcast_to(jnp.asarray(zero, part.dtype), part.shape),
        shard,
        identity,
    )

    def turn(k, before):
        at = length - 1 - k if reverse else k
        reached = at > here if reverse else at < here
        new = combine(before, jax.tree.map(lambda part: part[at], everything))
        return jax.tree.map(lambda a, b: jnp.where(reached, a, b), new, before)

    return lax.fori_loop(0, length, turn, start)


def feature_map(raw):
    return jax.nn.elu(raw) + 1.0


def feature_slope(raw):
    return jnp.where(raw > 0, 1.0, jnp.exp(raw))


def fdot(left, right):
    return jnp.dot(left, right, precision=highest, preferred_element_type=jnp.float32)


def add_pair(earlier, later):
    return (earlier[0] + later[0], earlier[1] + later[1])


def body(events, w_proj, targets, negatives, owners, item_rows):
    length = events.shape[0]
    size_head = events.shape[1]
    width = size_head * lax.axis_size("head")
    neg_count = negatives.shape[0]
    scale = 1.0 / math.sqrt(width)
    line = lax.iota(jnp.int32, length)
    causal = (line[:, None] >= line[None, :]).astype(jnp.float32)
    raw_query = jnp.dot(events, w_proj[0], preferred_element_type=jnp.float32)
    raw_key = jnp.dot(events, w_proj[1], preferred_element_type=jnp.float32)
    value_rows = jnp.dot(events, w_proj[2], preferred_element_type=jnp.float32)
    query_map = feature_map(raw_query)
    key_map = feature_map(raw_key)
    local_state = fdot(key_map.T, value_rows)
    local_total = jnp.sum(key_map, axis=0, keepdims=True)
    zero_state = jnp.zeros((size_head, size_head), jnp.float32)
    zero_total = jnp.zeros((1, size_head), jnp.float32)
    state_in, total_in = carried_in(
        (local_state, local_total), "ctx", add_pair, (zero_state, zero_total), False
    )
    scores = fdot(query_map, key_map.T) * causal
    numer = fdot(scores, value_rows) + fdot(query_map, state_in)
    denom = jnp.sum(scores, axis=1) + jnp.sum(query_map * total_in, axis=1)
    attended = numer / denom[:, None]
    mixed = (events.astype(jnp.float32) + attended).astype(jnp.bfloat16)
    neg_part = jnp.dot(mixed, negatives.T, preferred_element_type=jnp.float32)
    pos_part = jnp.sum(mixed.astype(jnp.float32) * targets.astype(jnp.float32), axis=1)
    neg_full, pos_full = lax.psum((neg_part, pos_part), "head")
    sigma = jax.nn.sigmoid(neg_full * scale - (pos_full * scale)[:, None])
    weight_b = (sigma / neg_count).astype(jnp.bfloat16)
    coeff = jnp.sum(sigma, axis=1) / neg_count
    grad_out = jnp.dot(weight_b, negatives, preferred_element_type=jnp.float32) - coeff[
        :, None
    ] * targets.astype(jnp.float32)
    d_num = grad_out / denom[:, None]
    d_den = -jnp.sum(grad_out * attended, axis=1) / denom
    local_adj = fdot(query_map.T, d_num)
    local_adjt = fdot(d_den[None, :], query_map)
    adj_state, adj_total = carried_in(
        (local_adj, local_adjt), "ctx", add_pair, (zero_state, zero_total), True
    )
    weight_mat = (fdot(d_num, value_rows.T) + d_den[:, None]) * causal
    d_values = fdot(key_map, adj_state) + fdot(scores.T, d_num)
    d_keys = fdot(value_rows, adj_state.T) + adj_total + fdot(weight_mat.T, query_map)
    d_query = fdot(d_num, state_in.T) + d_den[:, None] * total_in + fdot(weight_mat, key_map)
    weights_f = w_proj.astype(jnp.float32)
    grad_events = grad_out + fdot(d_query * feature_slope(raw_query), weights_f[0].T)
    grad_events = grad_events + fdot(d_keys * feature_slope(raw_key), weights_f[1].T)
    grad_events = grad_events + fdot(d_values, weights_f[2].T)
    grad_b = grad_events.astype(jnp.bfloat16)
    ctx_count = lax.axis_size("ctx")
    capacity = 3 * length // (2 * ctx_count)
    owner_list = owners[:, 0]
    owner_hot = (owner_list[:, None] == lax.iota(jnp.int32, ctx_count)[None, :]).astype(jnp.int32)
    earlier_count = jnp.cumsum(owner_hot, axis=0) - owner_hot
    rank_within = jnp.sum(earlier_count * owner_hot, axis=1)
    slot_index = owner_list * capacity + rank_within
    placing = slot_index[None, :] == lax.iota(jnp.int32, ctx_count * capacity)[:, None]
    send_rows = jnp.dot(
        placing.astype(jnp.bfloat16), grad_b, preferred_element_type=jnp.float32
    ).astype(jnp.bfloat16)
    send_ids = jnp.sum(jnp.where(placing, item_rows[None, :] + 1, 0), axis=1)
    recv_rows, recv_ids = (
        lax.all_to_all(
            send_rows.reshape(ctx_count, capacity, size_head),
            "ctx",
            split_axis=0,
            concat_axis=0,
            tiled=True,
        ),
        lax.all_to_all(
            send_ids.reshape(ctx_count, capacity), "ctx", split_axis=0, concat_axis=0, tiled=True
        ),
    )
    picking = (recv_ids.reshape(-1)[None, :] - 1 == lax.iota(jnp.int32, ROWS_OWN)[:, None]).astype(
        jnp.bfloat16
    )
    table_grad = jnp.dot(
        picking,
        recv_rows.reshape(ctx_count * capacity, size_head),
        preferred_element_type=jnp.float32,
    )
    return table_grad


def solution(mesh):
    placed = (
        P("ctx", "head"),
        P(None, "head", None),
        P("ctx", "head"),
        P(None, "head"),
        P("ctx", None),
        P("ctx"),
    )
    return jax.shard_map(
        body, mesh=mesh, in_specs=placed, out_specs=P("ctx", "head"), check_vma=False
    )
```

profile of v0, /device:TPU:0, one launch (start us, length us, event | category | flops | bytes accessed | tf_op | source)
XLA Modules:
  0.0 193.6 jit_solution(2406032428216903425)
XLA Ops:
  6.6 1.0 copy.35
  7.6 1.2 fusion.37
  8.7 1.0 fusion.15
  9.7 0.9 copy.39
  10.7 0.3 fusion.38
  11.0 33.1 %all-gather = f32[1024,128]{1,0:T(8,128)S(1)} all-gather(f32[128,128]{1,0:T(8,128)S(1)} %fusion.38), channel_id=2, replica_groups=mesh['ctx'=8,'head'=4] {'ctx'}, dimensions={0}, use_global_device_ids=true | all-gather | bytes 589824 | tf_op jit(solution)/shard_map/all_gather | solution.py:16
  44.1 20.5 %all-gather.4 = f32[8,1,128]{2,1,0:T(1,128)S(1)} all-gather(f32[1,1,128]{2,1,0:T(1,128)S(1)} %bitcast.90), channel_id=3, replica_groups=mesh['ctx'=8,'head'=4] {'ctx'}, dimensions={0}, use_global_device_ids=true | all-gather | bytes 4608 | tf_op jit(solution)/shard_map/all_gather | solution.py:16
  64.5 0.5 while.34
  65.0 0.3 multiply_reduce_fusion.1
  65.3 0.5 fusion.49
  65.8 0.3 fusion.45
  66.2 0.4 fusion.9
  66.6 0.0 copy-done
  66.6 0.0 copy-start.4
  66.6 0.0 copy-start.5
  66.6 1.7 fusion.33
  68.3 0.0 all-reduce.2.cloned.1.call-update
  68.4 0.6 reduce-window.6
  69.0 0.2 slice_reduce_fusion
  69.2 0.1 fusion.30
  69.4 0.1 select_reduce_fusion
  69.5 0.7 all_to_all.9
  70.2 3.3 %all-to-all-start = ((s32[8,1,48]{2,1,0:T(1,128)}), s32[8,1,48]{2,1,0:T(1,128)S(1)}, u32[]{:S(2)}, u32[]{:S(2)}) async-start(s32[8,1,48]{2,1,0:T(1,128)} %all_to_all.9), calls=%async_computation | async-start | bytes 8192 | tf_op jit(solution)/shard_map/all_to_all | solution.py:118
  73.5 6.4 %psum.15 = f32[256]{0:T(256)S(1)} all-reduce(f32[256]{0:T(256)S(1)} %get-tuple-element.346), channel_id=1, replica_groups=mesh['ctx'=8,'head'=4] {'head'}, use_global_device_ids=true, to_apply=%region_11.12 | all-reduce | flops 256 | bytes 2048 | tf_op jit(solution)/shard_map/psum | solution.py:75
  79.9 35.3 %all-reduce.2.cloned.1.call-done = f32[256,1920]{1,0:T(8,128)} async-done(((f32[256,1920]{1,0:T(8,128)}), f32[256,1920]{1,0:T(8,128)}) %all-reduce.2.cloned.1.call-update) | async-done | bytes 1966096 | tf_op jit(solution)/shard_map/psum | solution.py:75
  115.2 2.4 %fusion.48 = f32[256]{0:T(256)S(1)} fusion(f32[256]{0:T(256)S(1)} %broadcast_multiply_fusion.1, f32[256,1920]{1,0:T(8,128)} %all-reduce.2.cloned.1.call-done), kind=kLoop, calls=%fused_computation.87 | loop fusion | flops 2948864 | bytes 1968128 | tf_op jit(solution)/shard_map/reduce_sum | solution.py:78
  117.6 0.8 multiply_reduce_fusion
  118.4 0.3 convolution_add_fusion.9
  118.7 0.4 fusion
  119.1 0.3 fusion.43
  119.4 0.3 fusion.2
  119.7 0.2 convolution_add_fusion.8
  120.0 31.4 %all-gather.2 = f32[1024,128]{1,0:T(8,128)S(1)} all-gather(f32[128,128]{1,0:T(8,128)S(1)} %fusion.43), channel_id=4, replica_groups=mesh['ctx'=8,'head'=4] {'ctx'}, dimensions={0}, use_global_device_ids=true | all-gather | bytes 589824 | tf_op jit(solution)/shard_map/all_gather | solution.py:16
  151.3 0.2 convolution_bitcast_fusion
  151.5 20.5 %all-gather.5 = f32[8,1,128]{2,1,0:T(1,128)S(1)} all-gather(f32[1,1,128]{2,1,0:T(1,128)S(1)} %convolution_bitcast_fusion), channel_id=5, replica_groups=mesh['ctx'=8,'head'=4] {'ctx'}, dimensions={0}, use_global_device_ids=true | all-gather | bytes 4608 | tf_op jit(solution)/shard_map/all_gather | solution.py:16
  172.0 0.5 while.35
  172.5 0.4 fusion.34
  173.0 0.3 convolution_add_fusion.7
  173.2 0.4 fusion.1
  173.6 0.4 convolution_add_fusion.1
  174.0 0.2 convolution_add_fusion.6
  174.3 0.2 fusion.4
  174.5 0.9 convolution_convert_fusion
  175.4 0.0 all-to-all-done
  175.4 3.4 %all-to-all-start.1 = ((bf16[8,48,128]{2,1,0:T(8,128)(2,1)}), bf16[8,48,128]{2,1,0:T(8,128)(2,1)S(1)}, u32[]{:S(2)}, u32[]{:S(2)}) async-start(bf16[8,48,128]{2,1,0:T(8,128)(2,1)} %bitcast.15), calls=%async_computation.1 | async-start | bytes 196608 | tf_op jit(solution)/shard_map/all_to_all | solution.py:111
  178.7 0.1 sub.32
  178.8 7.0 %all-to-all-done.1 = bf16[8,48,128]{2,1,0:T(8,128)(2,1)S(1)} async-done(((bf16[8,48,128]{2,1,0:T(8,128)(2,1)}), bf16[8,48,128]{2,1,0:T(8,128)(2,1)S(1)}, u32[]{:S(2)}, u32[]{:S(2)}) %all-to-all-start.1) | async-done | bytes 98336 | tf_op jit(solution)/shard_map/all_to_all | solution.py:111
  185.8 1.0 fusion.6
  (55 shorter events, 0.6 us)
Async XLA Ops:
  6.5 60.0 %copy-start = (bf16[1920,128]{1,0:T(8,128)(2,1)S(1)}, bf16[1920,128]{1,0:T(8,128)(2,1)}, u32[]{:S(2)}) copy-start(bf16[1920,128]{1,0:T(8,128)(2,1)} %param.13) | copy-start | bytes 1474564
  6.5 58.5 %copy-start.2 = (bf16[256,128]{1,0:T(8,128)(2,1)S(1)}, bf16[256,128]{1,0:T(8,128)(2,1)}, u32[]{:S(2)}) copy-start(bf16[256,128]{1,0:T(8,128)(2,1)} %param.10) | copy-start | bytes 196612
  6.5 58.5 %copy-start.3 = (bf16[3,128,128]{2,1,0:T(8,128)(2,1)S(1)}, bf16[3,128,128]{2,1,0:T(8,128)(2,1)}, u32[]{:S(2)}) copy-start(bf16[3,128,128]{2,1,0:T(8,128)(2,1)} %param.11) | copy-start | bytes 294916
  6.5 108.6 %all-reduce.2.cloned.1.call-start = ((), (), s32[]{:S(2)}) async-start(), calls=%async_computation.2 | async-start | bytes 3932160 | tf_op jit(solution)/shard_map/psum | solution.py:75
  66.6 1.8 copy-start.4
  66.6 2.7 %copy-start.5 = (s32[256]{0:T(256)S(1)}, s32[256]{0:T(256)}, u32[]{:S(2)}) copy-start(s32[256]{0:T(256)} %param.15) | copy-start | bytes 3076
  70.2 105.2 %all-to-all-start = ((s32[8,1,48]{2,1,0:T(1,128)}), s32[8,1,48]{2,1,0:T(1,128)S(1)}, u32[]{:S(2)}, u32[]{:S(2)}) async-start(s32[8,1,48]{2,1,0:T(1,128)} %all_to_all.9), calls=%async_computation | async-start | bytes 8192 | tf_op jit(solution)/shard_map/all_to_all | solution.py:118
  115.2 2.4 %copy-start.1 = (f32[256,1920]{1,0:T(8,128)S(1)}, f32[256,1920]{1,0:T(8,128)}, u32[]{:S(2)}) copy-start(f32[256,1920]{1,0:T(8,128)} %all-reduce.2.cloned.1.call-done) | copy-start | bytes 5898244
  175.4 10.4 %all-to-all-start.1 = ((bf16[8,48,128]{2,1,0:T(8,128)(2,1)}), bf16[8,48,128]{2,1,0:T(8,128)(2,1)S(1)}, u32[]{:S(2)}, u32[]{:S(2)}) async-start(bf16[8,48,128]{2,1,0:T(8,128)(2,1)} %bitcast.15), calls=%async_computation.1 | async-start | bytes 196608 | tf_op jit(solution)/shard_map/all_to_all | solution.py:111
Sparse Core Ops, SparseCore 0:
  68.5 46.6 all-reduce.1
where the time goes:
time: 194 us
  blocking collectives  112 us (58%)
  waiting for transfers between devices  42.3 us (22%)
  between operations  13.7 us (7%)
  matrix products  12 us (6%)
  starting transfers between devices  6.64 us (3%)
  other arithmetic  3.75 us (2%)
  local copies, waits for them, and re-layouts  2.94 us (2%)
    all_gather x4, blocking collectives, carried_in(): everything = jax.tree.map(lambda part: lax.all_gather(part, axis), shard)  105 us
    psum x1, waiting for transfers between devices, body(): neg_full, pos_full = lax.psum((neg_part, pos_part), 'head')  35.3 us
    all_to_all x1, waiting for transfers between devices, body(): lax.all_to_all(send_rows.reshape(ctx_count, capacity, size_head), 'ctx',...  6.96 us
    psum x1, blocking collectives, body(): neg_full, pos_full = lax.psum((neg_part, pos_part), 'head')  6.37 us
    dot_general x16, matrix products, fdot(): jnp.dot(left, right, precision=highest, preferred_element_type=jnp.float32)  5.18 us
  transfers between devices with their start and end apart: 3, of which 2 were waited for; matrix products, arithmetic and copies ran while one was open for 5% of the time, Pallas kernels for 0%

commit v1 on v0

v1 whole, which is shorter than its diff:
```python
import functools
import math

import jax
import jax.numpy as jnp
from jax import lax
from jax.experimental import pallas as pl
from jax.experimental.pallas import tpu as pltpu
from jax.sharding import PartitionSpec as P

ROWS_OWN = 512
MESH = pl.DeviceIdType.MESH
F32 = jnp.float32
BF = jnp.bfloat16


def split_ctx(n):
    inner = 1
    while n % (inner * 2) == 0 and inner * inner * 4 <= n:
        inner *= 2
    return n // inner, inner


def mm(a, b, ca=1, cb=0):
    return lax.dot_general(
        a.astype(BF), b.astype(BF), (((ca,), (cb,)), ((), ())), preferred_element_type=F32
    )


def times(n, step):
    if n <= 16:
        for k in range(1, n):
            step(k)
    else:

        @pl.loop(1, n)
        def _(k):
            step(k)


def kernel(
    n_ctx, n_head, capacity, pieces,
    ev_ref, w_ref, tg_ref, neg_hbm, own_ref, item_ref,
    out_ref,
    negs, mixes, poss, ids_send, ids_recv, rows_send, rows_recv,
    state_own, state_in, state_mid, state_mid_in,
    adj_own, adj_in, adj_mid, adj_mid_in,
    acc, sums,
    sem_local, sem_ids, sem_neg, sem_fwd, sem_mix, sem_pos,
    sem_st, sem_st2, sem_ad, sem_ad2, sem_rows,
):
    outer, inner = split_ctx(n_ctx)
    length, size = ev_ref.shape
    neg_count = neg_hbm.shape[0]
    scale = 1.0 / math.sqrt(size * n_head)
    pairs = n_head // 2
    me = lax.axis_index("ctx")
    a, b = me // inner, me % inner
    h = lax.axis_index("head")
    p, c = h // 2, h % 2
    mate = p * 2 + (1 - c)

    barrier = pltpu.get_barrier_semaphore()

    def greet_ctx(k):
        pl.semaphore_signal(
            barrier, inc=1, device_id={"ctx": (me + k) % n_ctx}, device_id_type=MESH
        )

    def greet_head(k):
        pl.semaphore_signal(
            barrier, inc=1, device_id={"head": (h + k) % n_head}, device_id_type=MESH
        )

    times(n_ctx, greet_ctx)
    times(n_head, greet_head)

    def remote(src, dst, send, recv, **where):
        return pltpu.make_async_remote_copy(
            src_ref=src, dst_ref=dst, send_sem=send, recv_sem=recv,
            device_id=where, device_id_type=MESH,
        )

    local_neg = pltpu.make_async_copy(neg_hbm, negs.at[h], sem_local)
    local_neg.start()

    ev = ev_ref[...]
    raw_k = mm(ev, w_ref[1])
    val = mm(ev, w_ref[2])
    slope_k = jnp.exp(jnp.minimum(raw_k, 0.0))
    km = slope_k + jnp.maximum(raw_k, 0.0)
    own_rows = state_own.shape[0]
    line_pad = lax.broadcasted_iota(jnp.int32, (own_rows - size, size), 0)

    def pack(mat, row):
        tail = jnp.where(line_pad == 0, jnp.broadcast_to(row, line_pad.shape), 0.0)
        return jnp.concatenate([mat, tail], axis=0)

    own_state = pack(mm(km, val, 0, 0), jnp.sum(km, axis=0, keepdims=True))
    state_own[...] = own_state.astype(BF)

    pl.semaphore_wait(barrier, n_ctx - 1 + n_head - 1)

    def outer_copy(own, slots, sem, k, forward):
        to = a + k if forward else a - k
        return remote(own, slots.at[k], sem.at[0, k], sem.at[1, k], ctx=to * inner + b)

    def outer_there(k, forward):
        return a + k < outer if forward else a - k >= 0

    def outer_start(own, slots, sem, forward):
        def step(k):
            @pl.when(outer_there(k, forward))
            def _():
                outer_copy(own, slots, sem, k, forward).start()

        times(outer, step)

    def outer_sum(own, slots, sem, forward):
        acc[...] = jnp.zeros_like(acc)

        def step(k):
            @pl.when(outer_there(k, not forward))
            def _():
                outer_copy(own, slots, sem, k, not forward).wait_recv()
                acc[...] += slots[k].astype(F32)

        times(outer, step)

    def outer_end(own, slots, sem, forward):
        def step(k):
            @pl.when(outer_there(k, forward))
            def _():
                outer_copy(own, slots, sem, k, forward).wait_send()

        times(outer, step)

    def inner_copy(mids, slots, sem, j):
        to = a * inner + (b + j) % inner
        return remote(mids.at[j], slots.at[j], sem.at[0, j], sem.at[1, j], ctx=to)

    def inner_start(own_value, mids, slots, sem, forward):
        def step(j):
            to = (b + j) % inner
            passed = b < to if forward else b > to
            mids[j] = (acc[...] + jnp.where(passed, own_value, 0.0)).astype(BF)
            inner_copy(mids, slots, sem, j).start()

        times(inner, step)

    def inner_sum(mids, slots, sem):
        def step(j):
            inner_copy(mids, slots, sem, j).wait()
            acc[...] += slots[j].astype(F32)

        times(inner, step)

    outer_start(state_own, state_in, sem_st, True)

    piece = neg_count // pieces

    def neg_copy(slot, i, to, send, recv, source=None):
        rows = pl.ds(i * piece, piece)
        src = negs.at[slot, rows] if source is None else source.at[rows]
        return remote(src, negs.at[slot, rows], send, recv, head=to)

    def neg_far(i, k):
        to = ((p + k) % pairs) * 2 + c
        return neg_copy(h, i, to, sem_neg.at[0, k, i], sem_neg.at[1, k, i], neg_hbm)

    def neg_near(i):
        return neg_copy(h, i, mate, sem_neg.at[0, 0, i], sem_neg.at[1, 0, i], neg_hbm)

    def neg_from_far(i, k):
        slot = ((p - k + pairs) % pairs) * 2 + c
        return neg_copy(slot, i, mate, sem_neg.at[0, k, i], sem_neg.at[1, k, i])

    def neg_pass(i, k):
        slot = ((p - k + pairs) % pairs) * 2 + c
        return neg_copy(slot, i, mate, sem_fwd.at[0, k, i], sem_fwd.at[1, k, i])

    for i in range(pieces):
        for k in range(1, pairs):
            neg_far(i, k).start()
    for i in range(pieces):
        neg_near(i).start()

    raw_q = mm(ev, w_ref[0])
    slope_q = jnp.exp(jnp.minimum(raw_q, 0.0))
    qm = slope_q + jnp.maximum(raw_q, 0.0)
    at_row = lax.broadcasted_iota(jnp.int32, (length, length), 0)
    at_col = lax.broadcasted_iota(jnp.int32, (length, length), 1)
    causal = at_row >= at_col
    scores = jnp.where(causal, mm(qm, km, 1, 1), 0.0)
    scores_b = scores.astype(BF)
    numer = mm(scores_b, val)
    denom = jnp.sum(scores, axis=1, keepdims=True)

    outer_sum(state_own, state_in, sem_st, True)
    inner_start(own_state, state_mid, state_mid_in, sem_st2, True)

    lanes = ids_send.shape[2]
    hot = own_ref[...] == lax.broadcasted_iota(jnp.int32, (length, lanes), 1)
    hot_f = hot.astype(F32)
    earlier = mm((at_row > at_col).astype(F32), hot_f)
    rank = jnp.sum(earlier * hot_f, axis=1, keepdims=True).astype(jnp.int32)
    rank_hot = (rank == lax.broadcasted_iota(jnp.int32, (length, lanes), 1)).astype(F32)
    number = item_ref[...] + 1
    hot_t = hot_f.T
    high = mm(hot_t * (number // 16).astype(F32), rank_hot)
    low = mm(hot_t * (number % 16).astype(F32), rank_hot)
    numbers = (high * 16.0 + low).astype(jnp.int32)
    for d in range(n_ctx):
        ids_send[d] = numbers[d : d + 1, :]

    def ids_copy(k):
        to = (me + k) % n_ctx
        return remote(
            ids_send.at[to], ids_recv.at[me], sem_ids.at[0, k], sem_ids.at[1, k], ctx=to
        )

    def ids_from(k):
        at = (me - k + n_ctx) % n_ctx
        return remote(
            ids_send.at[at], ids_recv.at[at], sem_ids.at[0, k], sem_ids.at[1, k], ctx=at
        )

    times(n_ctx, lambda k: ids_copy(k).start())
    ids_recv[me] = ids_send[me]
    slot = own_ref[...] * capacity + rank
    placing = (
        slot == lax.broadcasted_iota(jnp.int32, (length, n_ctx * capacity), 1)
    ).astype(F32).astype(BF)

    inner_sum(state_mid, state_mid_in, sem_st2)
    state = acc[0:size, :]
    total = acc[size : size + 1, :]
    state_b = state.astype(BF)

    numer = numer + mm(qm, state_b)
    denom = denom + jnp.sum(qm * total, axis=1, keepdims=True)
    inverse = 1.0 / denom
    att = numer * inverse
    mixed = (ev.astype(F32) + att).astype(BF)
    mixes[h] = mixed

    def mix_copy(k):
        to = (h + k) % n_head
        return remote(mixes.at[h], mixes.at[h], sem_mix.at[0, k], sem_mix.at[1, k], head=to)

    def mix_from(k):
        at = (h - k + n_head) % n_head
        return remote(mixes.at[at], mixes.at[at], sem_mix.at[0, k], sem_mix.at[1, k], head=at)

    def pos_copy(k):
        to = (h + k) % n_head
        return remote(poss.at[h], poss.at[h], sem_pos.at[0, k], sem_pos.at[1, k], head=to)

    def pos_from(k):
        at = (h - k + n_head) % n_head
        return remote(poss.at[at], poss.at[at], sem_pos.at[0, k], sem_pos.at[1, k], head=at)

    for k in range(1, n_head):
        mix_copy(k).start()
    targets = tg_ref[...].astype(F32)
    pos = jnp.sum(mixed.astype(F32) * targets, axis=1, keepdims=True)
    poss[h] = jnp.broadcast_to(pos, (length, size)).T[0:8, :]
    for k in range(1, n_head):
        pos_copy(k).start()

    for i in range(pieces):
        for k in range(1, pairs):
            neg_from_far(i, k).wait_recv()
            neg_pass(i, k).start()
    for k in range(1, n_head):
        mix_from(k).wait_recv()
        pos_from(k).wait_recv()
    local_neg.wait()

    pos_all = poss[0]
    for k in range(1, n_head):
        pos_all = pos_all + poss[k]
    pos_col = pos_all.T[:, 0:1] * (0.5 * scale)
    mixed_all = jnp.concatenate([mixes[k] for k in range(n_head)], axis=1)

    grad = jnp.zeros((length, size), F32)
    coef = jnp.zeros((length, 1), F32)
    for i in range(pieces):
        rows = pl.ds(i * piece, piece)
        neg_near(i).wait_recv()
        for k in range(1, pairs):
            neg_pass(i, k).wait_recv()
        block = jnp.concatenate([negs[k, rows] for k in range(n_head)], axis=1)
        score = mm(mixed_all, block, 1, 1)
        sigma = 0.5 + 0.5 * jnp.tanh(score * (0.5 * scale) - pos_col)
        coef = coef + jnp.sum(sigma, axis=1, keepdims=True)
        grad = grad + mm((sigma * (1.0 / neg_count)).astype(BF), negs[h, rows])
    grad = grad - (coef * (1.0 / neg_count)) * targets

    d_num = grad * inverse
    d_den = -jnp.sum(grad * att, axis=1, keepdims=True) * inverse
    d_num_b = d_num.astype(BF)
    qm_b = qm.astype(BF)
    own_adj = pack(mm(qm_b, d_num_b, 0, 0), jnp.sum(d_den * qm, axis=0, keepdims=True))
    adj_own[...] = own_adj.astype(BF)
    outer_start(adj_own, adj_in, sem_ad, False)

    weight = jnp.where(causal, mm(d_num_b, val, 1, 1) + d_den, 0.0).astype(BF)
    d_val = mm(scores_b, d_num_b, 0, 0)
    d_key = mm(weight, qm_b, 0, 0)
    d_query = mm(d_num_b, state_b, 1, 1) + d_den * total + mm(weight, km)
    grad = grad + mm(d_query * slope_q, w_ref[0], 1, 1)

    outer_sum(adj_own, adj_in, sem_ad, False)
    inner_start(own_adj, adj_mid, adj_mid_in, sem_ad2, False)

    times(n_ctx, lambda k: ids_from(k).wait_recv())
    numbers = jnp.concatenate([ids_recv[s][:, 0:capacity] for s in range(n_ctx)], axis=1)
    picking = (
        numbers - 1
        == lax.broadcasted_iota(jnp.int32, (ROWS_OWN, n_ctx * capacity), 0)
    ).astype(F32).astype(BF)

    inner_sum(adj_mid, adj_mid_in, sem_ad2)
    adj = acc[0:size, :].astype(BF)
    adj_total = acc[size : size + 1, :]
    d_val = d_val + mm(km, adj)
    d_key = d_key + mm(val, adj, 1, 1) + adj_total
    grad = grad + mm(d_key * slope_k, w_ref[1], 1, 1) + mm(d_val, w_ref[2], 1, 1)
    placed = mm(placing, grad.astype(BF), 0, 0).astype(BF)
    rows_send[...] = placed.reshape(n_ctx, capacity, size)

    def rows_copy(k):
        to = (me + k) % n_ctx
        return remote(
            rows_send.at[to], rows_recv.at[me], sem_rows.at[0, k], sem_rows.at[1, k], ctx=to
        )

    def rows_from(k):
        at = (me - k + n_ctx) % n_ctx
        return remote(
            rows_send.at[at], rows_recv.at[at], sem_rows.at[0, k], sem_rows.at[1, k], ctx=at
        )

    times(n_ctx, lambda k: rows_copy(k).start())
    rows_recv[me] = rows_send[me]

    outer_end(state_own, state_in, sem_st, True)
    outer_end(adj_own, adj_in, sem_ad, False)
    times(n_ctx, lambda k: ids_copy(k).wait_send())
    for k in range(1, n_head):
        mix_copy(k).wait_send()
        pos_copy(k).wait_send()
    for i in range(pieces):
        neg_near(i).wait_send()
        for k in range(1, pairs):
            neg_far(i, k).wait_send()
            neg_pass(i, k).wait_send()
    times(n_ctx, lambda k: rows_copy(k).wait_send())
    times(n_ctx, lambda k: rows_from(k).wait_recv())
    out_ref[...] = mm(picking, rows_recv[...].reshape(n_ctx * capacity, size))


def body(n_ctx, n_head, events, w_proj, targets, negatives, owners, item_rows):
    length, size = events.shape
    neg_count = negatives.shape[0]
    capacity = -(-(3 * length // (2 * n_ctx)) // 16) * 16
    outer, inner = split_ctx(n_ctx)
    pieces = 3
    packed = size + 16
    lanes = max(128, n_ctx)
    dma = pltpu.SemaphoreType.DMA
    vmem = pl.BlockSpec(memory_space=pltpu.VMEM)
    scans = [
        pltpu.VMEM((packed, size), BF),
        pltpu.VMEM((outer, packed, size), BF),
        pltpu.VMEM((max(inner, 2), packed, size), BF),
        pltpu.VMEM((max(inner, 2), packed, size), BF),
    ]
    return pl.pallas_call(
        functools.partial(kernel, n_ctx, n_head, capacity, pieces),
        out_shape=jax.ShapeDtypeStruct((ROWS_OWN, size), F32),
        in_specs=[vmem, vmem, vmem, pl.BlockSpec(memory_space=pl.ANY), vmem, vmem],
        out_specs=vmem,
        scratch_shapes=[
            pltpu.VMEM((n_head, neg_count, size), BF),
            pltpu.VMEM((n_head, length, size), BF),
            pltpu.VMEM((n_head, 8, length), F32),
            pltpu.VMEM((n_ctx, 1, lanes), jnp.int32),
            pltpu.VMEM((n_ctx, 1, lanes), jnp.int32),
            pltpu.VMEM((n_ctx, capacity, size), BF),
            pltpu.VMEM((n_ctx, capacity, size), BF),
            *scans,
            *scans,
            pltpu.VMEM((packed, size), F32),
            pltpu.VMEM((8, 128), F32),
            dma,
            dma((2, n_ctx)),
            dma((2, n_head // 2, pieces)),
            dma((2, n_head // 2, pieces)),
            dma((2, n_head)),
            dma((2, n_head)),
            dma((2, outer)),
            dma((2, max(inner, 2))),
            dma((2, outer)),
            dma((2, max(inner, 2))),
            dma((2, n_ctx)),
        ],
        compiler_params=pltpu.CompilerParams(
            collective_id=0, has_side_effects=True, vmem_limit_bytes=48 * 1024 * 1024
        ),
    )(events, w_proj, targets, negatives, owners, item_rows.reshape(1, length))


def solution(mesh):
    placed = (
        P("ctx", "head"),
        P(None, "head", None),
        P("ctx", "head"),
        P(None, "head"),
        P("ctx", None),
        P("ctx"),
    )
    return jax.shard_map(
        functools.partial(body, mesh.shape["ctx"], mesh.shape["head"]),
        mesh=mesh, in_specs=placed, out_specs=P("ctx", "head"), check_vma=False,
    )
```

time: 194 us -> 41.6 us (0.21)
  blocking collectives: 112 us -> 0 us
  waiting for transfers between devices: 42.3 us -> 0 us
  Pallas kernels: 0 us -> 36.5 us
  between operations: 13.7 us -> 0.02 us
  matrix products: 12 us -> 0 us
  starting transfers between devices: 6.64 us -> 0 us
  other arithmetic: 3.75 us -> 0 us
    all_gather x4 -> x0, blocking collectives: 105 us -> none  [carried_in(): everything = jax.tree.map(lambda part: lax.all_gather(part, axis), shard)]
    pallas_call x0 -> x1, Pallas kernels: none -> 36.5 us  [body(): pl.pallas_call(functools.partial(kernel, n_ctx, n_head, capacity, pieces)...]
    psum x1 -> x0, waiting for transfers between devices: 35.3 us -> none  [body(): neg_full, pos_full = lax.psum((neg_part, pos_part), 'head')]
    dot_general x23 -> x0, matrix products: 12 us -> none  [the longest x16 5.18 us: fdot(): jnp.dot(left, right, precision=highest, preferred_element_type=jnp.float32)]
    all_to_all x2 -> x0, waiting for transfers between devices: 6.96 us -> none  [the longest x1 6.96 us: body(): lax.all_to_all(send_rows.reshape(ctx_count, capacity, size_head), 'ctx',...]
    all_to_all x2 -> x0, starting transfers between devices: 6.64 us -> none  [the longest x1 3.36 us: body(): lax.all_to_all(send_rows.reshape(ctx_count, capacity, size_head), 'ctx',...]
    psum x1 -> x0, blocking collectives: 6.37 us -> none  [body(): neg_full, pos_full = lax.psum((neg_part, pos_part), 'head')]
    unnamed x14, local copies, waits for them, and re-layouts: 1.97 us -> 4.77 us
  transfers between devices with their start and end apart: 3 -> 0, of which waited for: 2 -> 0; matrix products, arithmetic and copies ran while one was open for 5% -> 0% of each run, Pallas kernels for 0% -> 0%
where the time goes in v1:
time: 41.6 us; the launch traced here: 41.3 us
  Pallas kernels  36.5 us (88%)
  local copies, waits for them, and re-layouts  4.77 us (11%)
    pallas_call x1, Pallas kernels, body(): pl.pallas_call(functools.partial(kernel, n_ctx, n_head, capacity, pieces)...  36.5 us
    unnamed x14, local copies, waits for them, and re-layouts  4.77 us

profile of v1, /device:TPU:0, one launch (start us, length us, event | category | flops | bytes accessed | tf_op | source)
XLA Modules:
  0.0 41.3 jit_solution(14361471455849504703)
XLA Ops:
  0.0 0.0 copy-start.5
  0.0 0.0 copy-start.1
  0.0 0.7 %copy-done.5 = s32[256,1]{0,1:T(1,128)S(1)} copy-done((s32[256,1]{0,1:T(1,128)S(1)}, s32[256,1]{0,1:T(1,128)}, u32[]{:S(2)}) %copy-start.5) | copy-done | bytes 1048
  0.7 0.0 copy-start.4
  0.7 0.1 copy.7.own_ref
  0.8 0.1 copy-done.1
  0.9 0.5 %copy-done.4 = s32[256]{0:T(256)S(1)} copy-done((s32[256]{0:T(256)S(1)}, s32[256]{0:T(256)}, u32[]{:S(2)}) %copy-start.4) | copy-done | bytes 1048
  1.4 0.0 copy-start
  1.4 1.0 %copy-done = bf16[1920,128]{1,0:T(8,128)(2,1)S(1)} copy-done((bf16[1920,128]{1,0:T(8,128)(2,1)S(1)}, bf16[1920,128]{1,0:T(8,128)(2,1)}, u32[]{:S(2)}) %copy-start) | copy-done | bytes 491544
  2.4 0.0 copy-start.2
  2.4 0.8 %copy-done.2 = bf16[256,128]{1,0:T(8,128)(2,1)S(1)} copy-done((bf16[256,128]{1,0:T(8,128)(2,1)S(1)}, bf16[256,128]{1,0:T(8,128)(2,1)}, u32[]{:S(2)}) %copy-start.2) | copy-done | bytes 65560
  3.2 0.0 copy-start.3
  3.2 0.8 %copy-done.3 = bf16[256,128]{1,0:T(8,128)(2,1)S(1)} copy-done((bf16[256,128]{1,0:T(8,128)(2,1)S(1)}, bf16[256,128]{1,0:T(8,128)(2,1)}, u32[]{:S(2)}) %copy-start.3) | copy-done | bytes 65560
  4.1 36.5 %shard_map.64 = f32[512,128]{1,0:T(8,128)S(1)} custom-call(bf16[256,128]{1,0:T(8,128)(2,1)S(1)} %copy-done.2, bf16[3,128,128]{2,1,0:T(8,128)(2,1)S(1)} %copy-done.1, bf16[256,128]{1,0:T(8,128)(2,1)S(1)} %copy-done.3, bf16[1920,128]{1,0:T(8,128)(2,1)S(1)} %copy-done, s32[256,1]{1,0:T(8,128)S(1)} %copy.7.own_ref, s32[1,256]{1,0:T(1,128)S(1)} %bitcast.1), custom_call_target="tpu_custom_call" | custom-call | tf_op jit(solution)/shard_map/pallas_call | solution.py:380
  40.6 0.7 %copy.9 = f32[512,128]{1,0:T(8,128)} copy(f32[512,128]{1,0:T(8,128)S(1)} %shard_map.64) | data formatting | bytes 524288
Async XLA Ops:
  0.0 0.7 %copy-start.5 = (s32[256,1]{0,1:T(1,128)S(1)}, s32[256,1]{0,1:T(1,128)}, u32[]{:S(2)}) copy-start(s32[256,1]{0,1:T(1,128)} %param.10) | copy-start | bytes 3076
  0.0 0.9 %copy-start.1 = (bf16[3,128,128]{2,1,0:T(8,128)(2,1)S(1)}, bf16[3,128,128]{2,1,0:T(8,128)(2,1)}, u32[]{:S(2)}) copy-start(bf16[3,128,128]{2,1,0:T(8,128)(2,1)} %w_ref.1) | copy-start | bytes 294916
  0.7 0.7 %copy-start.4 = (s32[256]{0:T(256)S(1)}, s32[256]{0:T(256)}, u32[]{:S(2)}) copy-start(s32[256]{0:T(256)} %param.11) | copy-start | bytes 3076
  1.4 1.0 %copy-start = (bf16[1920,128]{1,0:T(8,128)(2,1)S(1)}, bf16[1920,128]{1,0:T(8,128)(2,1)}, u32[]{:S(2)}) copy-start(bf16[1920,128]{1,0:T(8,128)(2,1)} %neg_hbm.1) | copy-start | bytes 1474564
  2.4 0.8 %copy-start.2 = (bf16[256,128]{1,0:T(8,128)(2,1)S(1)}, bf16[256,128]{1,0:T(8,128)(2,1)}, u32[]{:S(2)}) copy-start(bf16[256,128]{1,0:T(8,128)(2,1)} %ev_ref.1) | copy-start | bytes 196612
  3.2 0.8 %copy-start.3 = (bf16[256,128]{1,0:T(8,128)(2,1)S(1)}, bf16[256,128]{1,0:T(8,128)(2,1)}, u32[]{:S(2)}) copy-start(bf16[256,128]{1,0:T(8,128)(2,1)} %tg_ref.1) | copy-start | bytes 196612

commit v2 on v1

--- a/solution.py
+++ b/solution.py
@@ -16,7 +16,7 @@
 
 def split_ctx(n):
     inner = 1
-    while n % (inner * 2) == 0 and inner * inner * 4 <= n:
+    while n % (inner * 2) == 0 and inner * inner * 2 <= n:
         inner *= 2
     return n // inner, inner
 
@@ -40,17 +40,18 @@
 
 def kernel(
     n_ctx, n_head, capacity, pieces,
-    ev_ref, w_ref, tg_ref, neg_hbm, own_ref, item_ref,
+    ev_hbm, w_hbm, tg_hbm, neg_hbm, own_hbm, item_hbm,
     out_ref,
+    ev_ref, w_ref, tg_ref, own_ref, item_ref,
     negs, mixes, poss, ids_send, ids_recv, rows_send, rows_recv,
     state_own, state_in, state_mid, state_mid_in,
     adj_own, adj_in, adj_mid, adj_mid_in,
-    acc, sums,
-    sem_local, sem_ids, sem_neg, sem_fwd, sem_mix, sem_pos,
+    acc,
+    sem_local, sem_ids, sem_near, sem_far, sem_cross, sem_pass, sem_mix, sem_pos,
     sem_st, sem_st2, sem_ad, sem_ad2, sem_rows,
 ):
     outer, inner = split_ctx(n_ctx)
-    length, size = ev_ref.shape
+    length, size = ev_hbm.shape
     neg_count = neg_hbm.shape[0]
     scale = 1.0 / math.sqrt(size * n_head)
     pairs = n_head // 2
@@ -81,8 +82,23 @@
             device_id=where, device_id_type=MESH,
         )
 
-    local_neg = pltpu.make_async_copy(neg_hbm, negs.at[h], sem_local)
-    local_neg.start()
+    loads = [
+        pltpu.make_async_copy(src, dst, sem_local.at[i])
+        for i, (src, dst) in enumerate(
+            (
+                (ev_hbm, ev_ref),
+                (w_hbm, w_ref),
+                (own_hbm, own_ref),
+                (item_hbm, item_ref),
+                (tg_hbm, tg_ref),
+                (neg_hbm, negs.at[h]),
+            )
+        )
+    ]
+    for load in loads:
+        load.start()
+    loads[0].wait()
+    loads[1].wait()
 
     ev = ev_ref[...]
     raw_k = mm(ev, w_ref[1])
@@ -157,33 +173,61 @@
 
     outer_start(state_own, state_in, sem_st, True)
 
-    piece = neg_count // pieces
-
-    def neg_copy(slot, i, to, send, recv, source=None):
-        rows = pl.ds(i * piece, piece)
-        src = negs.at[slot, rows] if source is None else source.at[rows]
-        return remote(src, negs.at[slot, rows], send, recv, head=to)
-
-    def neg_far(i, k):
+    parts = 2
+    piece = neg_count // (2 * parts)
+    half = me % 2
+    partner = me + 1 - 2 * half
+
+    def neg_rows(which, r):
+        return pl.ds(pl.multiple_of((which * parts + r) * piece, 16), piece)
+
+    def neg_slot(k):
+        return ((p - k + pairs) % pairs) * 2 + c
+
+    def neg_near():
+        return remote(neg_hbm, negs.at[h], sem_near.at[0], sem_near.at[1], head=mate)
+
+    def neg_far(k, r):
+        rows = neg_rows(half, r)
         to = ((p + k) % pairs) * 2 + c
-        return neg_copy(h, i, to, sem_neg.at[0, k, i], sem_neg.at[1, k, i], neg_hbm)
-
-    def neg_near(i):
-        return neg_copy(h, i, mate, sem_neg.at[0, 0, i], sem_neg.at[1, 0, i], neg_hbm)
-
-    def neg_from_far(i, k):
-        slot = ((p - k + pairs) % pairs) * 2 + c
-        return neg_copy(slot, i, mate, sem_neg.at[0, k, i], sem_neg.at[1, k, i])
-
-    def neg_pass(i, k):
-        slot = ((p - k + pairs) % pairs) * 2 + c
-        return neg_copy(slot, i, mate, sem_fwd.at[0, k, i], sem_fwd.at[1, k, i])
-
-    for i in range(pieces):
+        return remote(
+            neg_hbm.at[rows], negs.at[h, rows],
+            sem_far.at[0, k, r], sem_far.at[1, k, r], head=to,
+        )
+
+    def neg_from_far(k, r):
+        block = negs.at[neg_slot(k), neg_rows(half, r)]
+        return remote(block, block, sem_far.at[0, k, r], sem_far.at[1, k, r], head=neg_slot(k))
+
+    def neg_cross(k, r):
+        block = negs.at[neg_slot(k), neg_rows(half, r)]
+        return remote(block, block, sem_cross.at[0, k, r], sem_cross.at[1, k, r], ctx=partner)
+
+    def neg_from_cross(k, r):
+        block = negs.at[neg_slot(k), neg_rows(1 - half, r)]
+        return remote(block, block, sem_cross.at[0, k, r], sem_cross.at[1, k, r], ctx=partner)
+
+    def neg_pass(k, r, turn):
+        block = negs.at[neg_slot(k), neg_rows(half if turn == 0 else 1 - half, r)]
+        return remote(
+            block, block, sem_pass.at[0, k, r, turn], sem_pass.at[1, k, r, turn], head=mate
+        )
+
+    def neg_forward(r):
         for k in range(1, pairs):
-            neg_far(i, k).start()
-    for i in range(pieces):
-        neg_near(i).start()
+            neg_from_far(k, r).wait_recv()
+            neg_cross(k, r).start()
+            neg_pass(k, r, 0).start()
+
+    def neg_forward_cross(r):
+        for k in range(1, pairs):
+            neg_from_cross(k, r).wait_recv()
+            neg_pass(k, r, 1).start()
+
+    for r in range(parts):
+        for k in range(1, pairs):
+            neg_far(k, r).start()
+    neg_near().start()
 
     raw_q = mm(ev, w_ref[0])
     slope_q = jnp.exp(jnp.minimum(raw_q, 0.0))
@@ -200,15 +244,16 @@
     inner_start(own_state, state_mid, state_mid_in, sem_st2, True)
 
     lanes = ids_send.shape[2]
-    hot = own_ref[...] == lax.broadcasted_iota(jnp.int32, (length, lanes), 1)
-    hot_f = hot.astype(F32)
-    earlier = mm((at_row > at_col).astype(F32), hot_f)
-    rank = jnp.sum(earlier * hot_f, axis=1, keepdims=True).astype(jnp.int32)
-    rank_hot = (rank == lax.broadcasted_iota(jnp.int32, (length, lanes), 1)).astype(F32)
+    loads[2].wait()
+    loads[3].wait()
+    owner_row = own_ref[...]
+    hot = (owner_row == lax.broadcasted_iota(jnp.int32, (lanes, length), 0)).astype(F32)
+    earlier = mm(hot, (at_row < at_col).astype(F32))
+    rank = jnp.sum(earlier * hot, axis=0, keepdims=True).astype(jnp.int32)
+    rank_hot = (rank == lax.broadcasted_iota(jnp.int32, (lanes, length), 0)).astype(F32)
     number = item_ref[...] + 1
-    hot_t = hot_f.T
-    high = mm(hot_t * (number // 16).astype(F32), rank_hot)
-    low = mm(hot_t * (number % 16).astype(F32), rank_hot)
+    high = mm(hot * (number // 16).astype(F32), rank_hot, 1, 1)
+    low = mm(hot * (number % 16).astype(F32), rank_hot, 1, 1)
     numbers = (high * 16.0 + low).astype(jnp.int32)
     for d in range(n_ctx):
         ids_send[d] = numbers[d : d + 1, :]
@@ -227,11 +272,12 @@
 
     times(n_ctx, lambda k: ids_copy(k).start())
     ids_recv[me] = ids_send[me]
-    slot = own_ref[...] * capacity + rank
+    slot = owner_row * capacity + rank
     placing = (
-        slot == lax.broadcasted_iota(jnp.int32, (length, n_ctx * capacity), 1)
+        slot == lax.broadcasted_iota(jnp.int32, (n_ctx * capacity, length), 0)
     ).astype(F32).astype(BF)
 
+    neg_forward(0)
     inner_sum(state_mid, state_mid_in, sem_st2)
     state = acc[0:size, :]
     total = acc[size : size + 1, :]
@@ -262,20 +308,26 @@
 
     for k in range(1, n_head):
         mix_copy(k).start()
+    loads[4].wait()
     targets = tg_ref[...].astype(F32)
     pos = jnp.sum(mixed.astype(F32) * targets, axis=1, keepdims=True)
     poss[h] = jnp.broadcast_to(pos, (length, size)).T[0:8, :]
     for k in range(1, n_head):
         pos_copy(k).start()
 
-    for i in range(pieces):
-        for k in range(1, pairs):
-            neg_from_far(i, k).wait_recv()
-            neg_pass(i, k).start()
+    for r in range(1, parts):
+        neg_forward(r)
+    for r in range(parts):
+        neg_forward_cross(r)
     for k in range(1, n_head):
         mix_from(k).wait_recv()
         pos_from(k).wait_recv()
-    local_neg.wait()
+    loads[5].wait()
+    neg_near().wait_recv()
+    for k in range(1, pairs):
+        for r in range(parts):
+            neg_pass(k, r, 0).wait_recv()
+            neg_pass(k, r, 1).wait_recv()
 
     pos_all = poss[0]
     for k in range(1, n_head):
@@ -286,10 +338,7 @@
     grad = jnp.zeros((length, size), F32)
     coef = jnp.zeros((length, 1), F32)
     for i in range(pieces):
-        rows = pl.ds(i * piece, piece)
-        neg_near(i).wait_recv()
-        for k in range(1, pairs):
-            neg_pass(i, k).wait_recv()
+        rows = pl.ds(i * (neg_count // pieces), neg_count // pieces)
         block = jnp.concatenate([negs[k, rows] for k in range(n_head)], axis=1)
         score = mm(mixed_all, block, 1, 1)
         sigma = 0.5 + 0.5 * jnp.tanh(score * (0.5 * scale) - pos_col)
@@ -327,7 +376,7 @@
     d_val = d_val + mm(km, adj)
     d_key = d_key + mm(val, adj, 1, 1) + adj_total
     grad = grad + mm(d_key * slope_k, w_ref[1], 1, 1) + mm(d_val, w_ref[2], 1, 1)
-    placed = mm(placing, grad.astype(BF), 0, 0).astype(BF)
+    placed = mm(placing, grad.astype(BF)).astype(BF)
     rows_send[...] = placed.reshape(n_ctx, capacity, size)
 
     def rows_copy(k):
@@ -351,11 +400,13 @@
     for k in range(1, n_head):
         mix_copy(k).wait_send()
         pos_copy(k).wait_send()
-    for i in range(pieces):
-        neg_near(i).wait_send()
-        for k in range(1, pairs):
-            neg_far(i, k).wait_send()
-            neg_pass(i, k).wait_send()
+    neg_near().wait_send()
+    for k in range(1, pairs):
+        for r in range(parts):
+            neg_far(k, r).wait_send()
+            neg_cross(k, r).wait_send()
+            neg_pass(k, r, 0).wait_send()
+            neg_pass(k, r, 1).wait_send()
     times(n_ctx, lambda k: rows_copy(k).wait_send())
     times(n_ctx, lambda k: rows_from(k).wait_recv())
     out_ref[...] = mm(picking, rows_recv[...].reshape(n_ctx * capacity, size))
@@ -380,9 +431,14 @@
     return pl.pallas_call(
         functools.partial(kernel, n_ctx, n_head, capacity, pieces),
         out_shape=jax.ShapeDtypeStruct((ROWS_OWN, size), F32),
-        in_specs=[vmem, vmem, vmem, pl.BlockSpec(memory_space=pl.ANY), vmem, vmem],
+        in_specs=[pl.BlockSpec(memory_space=pltpu.HBM)] * 6,
         out_specs=vmem,
         scratch_shapes=[
+            pltpu.VMEM((length, size), BF),
+            pltpu.VMEM(w_proj.shape, BF),
+            pltpu.VMEM((length, size), BF),
+            pltpu.VMEM((1, length), jnp.int32),
+            pltpu.VMEM((1, length), jnp.int32),
             pltpu.VMEM((n_head, neg_count, size), BF),
             pltpu.VMEM((n_head, length, size), BF),
             pltpu.VMEM((n_head, 8, length), F32),
@@ -393,11 +449,12 @@
             *scans,
             *scans,
             pltpu.VMEM((packed, size), F32),
-            pltpu.VMEM((8, 128), F32),
-            dma,
+            dma((6,)),
             dma((2, n_ctx)),
-            dma((2, n_head // 2, pieces)),
-            dma((2, n_head // 2, pieces)),
+            dma((2,)),
+            dma((2, n_head // 2, 2)),
+            dma((2, n_head // 2, 2)),
+            dma((2, n_head // 2, 2, 2)),
             dma((2, n_head)),
             dma((2, n_head)),
             dma((2, outer)),
@@ -407,9 +464,16 @@
             dma((2, n_ctx)),
         ],
         compiler_params=pltpu.CompilerParams(
-            collective_id=0, has_side_effects=True, vmem_limit_bytes=48 * 1024 * 1024
+            collective_id=0, has_side_effects=True, vmem_limit_bytes=56 * 1024 * 1024
         ),
-    )(events, w_proj, targets, negatives, owners, item_rows.reshape(1, length))
+    )(
+        events,
+        w_proj,
+        targets,
+        negatives,
+        owners.reshape(1, length),
+        item_rows.reshape(1, length),
+    )
 
 
 def solution(mesh):

time: 41.6 us -> 34.5 us (0.83)
  Pallas kernels: 36.5 us -> 32.6 us
  local copies, waits for them, and re-layouts: 4.77 us -> 1.67 us
    pallas_call x1, Pallas kernels: 36.5 us -> 32.6 us  [body(): pl.pallas_call(functools.partial(kernel, n_ctx, n_head, capacity, pieces)...]
    unnamed x14 -> x1, local copies, waits for them, and re-layouts: 4.77 us -> 1.67 us
where the time goes in v2:
time: 34.5 us; the launch traced here: 34.3 us
  Pallas kernels  32.6 us (94%)
  local copies, waits for them, and re-layouts  1.67 us (5%)
    pallas_call x1, Pallas kernels, body(): pl.pallas_call(functools.partial(kernel, n_ctx, n_head, capacity, pieces)...  32.6 us
    unnamed x1, local copies, waits for them, and re-layouts  1.67 us

profile of v2, /device:TPU:0, one launch (start us, length us, event | category | flops | bytes accessed | tf_op | source)
XLA Modules:
  0.0 34.3 jit_solution(12922524113427637295)
XLA Ops:
  0.0 32.6 %shard_map.64 = f32[512,128]{1,0:T(8,128)} custom-call(bf16[256,128]{1,0:T(8,128)(2,1)} %ev_hbm.1, bf16[3,128,128]{2,1,0:T(8,128)(2,1)} %w_hbm.1, bf16[256,128]{1,0:T(8,128)(2,1)} %tg_hbm.1, bf16[1920,128]{1,0:T(8,128)(2,1)} %neg_hbm.1, s32[1,256]{1,0:T(1,128)} %bitcast.2, s32[1,256]{1,0:T(1,128)} %bitcast.3), custom_call_target="tpu_custom_call" | custom-call | tf_op jit(solution)/shard_map/pallas_call | solution.py:431
  32.7 1.7 %copy.8 = f32[512,128]{1,0:T(8,128)} copy(f32[512,128]{1,0:T(8,128)} %shard_map.64) | data formatting | bytes 524288

commit v3 on v2

--- a/solution.py
+++ b/solution.py
@@ -41,7 +41,7 @@
 def kernel(
     n_ctx, n_head, capacity, pieces,
     ev_hbm, w_hbm, tg_hbm, neg_hbm, own_hbm, item_hbm,
-    out_ref,
+    rows_out, numbers_out,
     ev_ref, w_ref, tg_ref, own_ref, item_ref,
     negs, mixes, poss, ids_send, ids_recv, rows_send, rows_recv,
     state_own, state_in, state_mid, state_mid_in,
@@ -117,59 +117,84 @@
 
     pl.semaphore_wait(barrier, n_ctx - 1 + n_head - 1)
 
-    def outer_copy(own, slots, sem, k, forward):
+    chunks = (pl.ds(0, 64), pl.ds(64, own_rows - 64))
+
+    def outer_copy(own, slots, sem, k, r, forward):
         to = a + k if forward else a - k
-        return remote(own, slots.at[k], sem.at[0, k], sem.at[1, k], ctx=to * inner + b)
+        rows = chunks[r]
+        return remote(
+            own.at[rows], slots.at[k, rows], sem.at[0, k, r], sem.at[1, k, r],
+            ctx=to * inner + b,
+        )
 
     def outer_there(k, forward):
         return a + k < outer if forward else a - k >= 0
 
     def outer_start(own, slots, sem, forward):
-        def step(k):
-            @pl.when(outer_there(k, forward))
-            def _():
-                outer_copy(own, slots, sem, k, forward).start()
-
-        times(outer, step)
-
-    def outer_sum(own, slots, sem, forward):
-        acc[...] = jnp.zeros_like(acc)
+        for r in range(len(chunks)):
+
+            def step(k):
+                @pl.when(outer_there(k, forward))
+                def _():
+                    outer_copy(own, slots, sem, k, r, forward).start()
+
+            times(outer, step)
+
+    def outer_sum(own, slots, sem, r, forward):
+        rows = chunks[r]
+        acc[rows] = jnp.zeros((rows.size, size), F32)
 
         def step(k):
             @pl.when(outer_there(k, not forward))
             def _():
-                outer_copy(own, slots, sem, k, not forward).wait_recv()
-                acc[...] += slots[k].astype(F32)
+                outer_copy(own, slots, sem, k, r, not forward).wait_recv()
+                acc[rows] += slots[k, rows].astype(F32)
 
         times(outer, step)
 
     def outer_end(own, slots, sem, forward):
-        def step(k):
-            @pl.when(outer_there(k, forward))
-            def _():
-                outer_copy(own, slots, sem, k, forward).wait_send()
-
-        times(outer, step)
-
-    def inner_copy(mids, slots, sem, j):
+        for r in range(len(chunks)):
+
+            def step(k):
+                @pl.when(outer_there(k, forward))
+                def _():
+                    outer_copy(own, slots, sem, k, r, forward).wait_send()
+
+            times(outer, step)
+
+    def inner_copy(mids, slots, sem, j, r):
         to = a * inner + (b + j) % inner
-        return remote(mids.at[j], slots.at[j], sem.at[0, j], sem.at[1, j], ctx=to)
-
-    def inner_start(own_value, mids, slots, sem, forward):
+        rows = chunks[r]
+        return remote(
+            mids.at[j, rows], slots.at[j, rows], sem.at[0, j, r], sem.at[1, j, r], ctx=to
+        )
+
+    def inner_start(own_value, mids, slots, sem, r, forward):
+        rows = chunks[r]
+        mine = own_value[rows.start : rows.start + rows.size]
+
         def step(j):
             to = (b + j) % inner
             passed = b < to if forward else b > to
-            mids[j] = (acc[...] + jnp.where(passed, own_value, 0.0)).astype(BF)
-            inner_copy(mids, slots, sem, j).start()
+            mids[j, rows] = (acc[rows] + jnp.where(passed, mine, 0.0)).astype(BF)
+            inner_copy(mids, slots, sem, j, r).start()
 
         times(inner, step)
 
     def inner_sum(mids, slots, sem):
-        def step(j):
-            inner_copy(mids, slots, sem, j).wait()
-            acc[...] += slots[j].astype(F32)
-
-        times(inner, step)
+        for r in range(len(chunks)):
+            rows = chunks[r]
+
+            def step(j):
+                inner_copy(mids, slots, sem, j, r).wait()
+                acc[rows] += slots[j, rows].astype(F32)
+
+            times(inner, step)
+
+    def scan_turn(own_value, own, slots, sem, mids, mid_slots, mid_sem, forward):
+        for r in range(len(chunks)):
+            outer_sum(own, slots, sem, r, forward)
+            inner_start(own_value, mids, mid_slots, mid_sem, r, forward)
 
     outer_start(state_own, state_in, sem_st, True)
 
@@ -240,8 +265,7 @@
     numer = mm(scores_b, val)
     denom = jnp.sum(scores, axis=1, keepdims=True)
 
-    outer_sum(state_own, state_in, sem_st, True)
-    inner_start(own_state, state_mid, state_mid_in, sem_st2, True)
+    scan_turn(own_state, state_own, state_in, sem_st, state_mid, state_mid_in, sem_st2, True)
 
     lanes = ids_send.shape[2]
     loads[2].wait()
@@ -360,15 +384,11 @@
     d_query = mm(d_num_b, state_b, 1, 1) + d_den * total + mm(weight, km)
     grad = grad + mm(d_query * slope_q, w_ref[0], 1, 1)
 
-    outer_sum(adj_own, adj_in, sem_ad, False)
-    inner_start(own_adj, adj_mid, adj_mid_in, sem_ad2, False)
+    scan_turn(own_adj, adj_own, adj_in, sem_ad, adj_mid, adj_mid_in, sem_ad2, False)
 
     times(n_ctx, lambda k: ids_from(k).wait_recv())
     numbers = jnp.concatenate([ids_recv[s][:, 0:capacity] for s in range(n_ctx)], axis=1)
-    picking = (
-        numbers - 1
-        == lax.broadcasted_iota(jnp.int32, (ROWS_OWN, n_ctx * capacity), 0)
-    ).astype(F32).astype(BF)
+    numbers_out[...] = numbers
 
     inner_sum(adj_mid, adj_mid_in, sem_ad2)
     adj = acc[0:size, :].astype(BF)
@@ -409,7 +429,15 @@
             neg_pass(k, r, 1).wait_send()
     times(n_ctx, lambda k: rows_copy(k).wait_send())
     times(n_ctx, lambda k: rows_from(k).wait_recv())
-    out_ref[...] = mm(picking, rows_recv[...].reshape(n_ctx * capacity, size))
+    rows_out[...] = rows_recv[...].reshape(n_ctx * capacity, size)
+
+
+def place_rows(rows_ref, numbers_ref, out_ref):
+    count = out_ref.shape[0]
+    first = pl.program_id(0) * count + 1
+    line = lax.broadcasted_iota(jnp.int32, (count, rows_ref.shape[0]), 0) + first
+    picking = (numbers_ref[...] == line).astype(F32).astype(BF)
+    out_ref[...] = mm(picking, rows_ref[...])
 
 
 def body(n_ctx, n_head, events, w_proj, targets, negatives, owners, item_rows):
@@ -428,11 +456,14 @@
         pltpu.VMEM((max(inner, 2), packed, size), BF),
         pltpu.VMEM((max(inner, 2), packed, size), BF),
     ]
-    return pl.pallas_call(
+    rows, numbers = pl.pallas_call(
         functools.partial(kernel, n_ctx, n_head, capacity, pieces),
-        out_shape=jax.ShapeDtypeStruct((ROWS_OWN, size), F32),
+        out_shape=(
+            jax.ShapeDtypeStruct((n_ctx * capacity, size), BF),
+            jax.ShapeDtypeStruct((1, n_ctx * capacity), jnp.int32),
+        ),
         in_specs=[pl.BlockSpec(memory_space=pltpu.HBM)] * 6,
-        out_specs=vmem,
+        out_specs=(vmem, vmem),
         scratch_shapes=[
             pltpu.VMEM((length, size), BF),
             pltpu.VMEM(w_proj.shape, BF),
@@ -457,10 +488,10 @@
             dma((2, n_head // 2, 2, 2)),
             dma((2, n_head)),
             dma((2, n_head)),
-            dma((2, outer)),
-            dma((2, max(inner, 2))),
-            dma((2, outer)),
-            dma((2, max(inner, 2))),
+            dma((2, outer, 2)),
+            dma((2, max(inner, 2), 2)),
+            dma((2, outer, 2)),
+            dma((2, max(inner, 2), 2)),
             dma((2, n_ctx)),
         ],
         compiler_params=pltpu.CompilerParams(
@@ -474,6 +505,18 @@
         owners.reshape(1, length),
         item_rows.reshape(1, length),
     )
+    blocks = 1
+    return pl.pallas_call(
+        place_rows,
+        grid=(blocks,),
+        out_shape=jax.ShapeDtypeStruct((ROWS_OWN, size), F32),
+        in_specs=[
+            pl.BlockSpec((n_ctx * capacity, size), lambda i: (0, 0)),
+            pl.BlockSpec((1, n_ctx * capacity), lambda i: (0, 0)),
+        ],
+        out_specs=pl.BlockSpec((ROWS_OWN // blocks, size), lambda i: (i, 0)),
+        compiler_params=pltpu.CompilerParams(vmem_limit_bytes=56 * 1024 * 1024),
+    )(rows, numbers)
 
 
 def solution(mesh):

time: 34.5 us -> 33.8 us (0.980)
  local copies, waits for them, and re-layouts: 1.67 us -> 0 us
  Pallas kernels: 32.6 us -> 33.7 us
    pallas_call x0 -> x1, Pallas kernels: none -> 1.87 us  [body(): pl.pallas_call(place_rows, grid=(blocks,), out_shape=jax.ShapeDtypeStruct...]
    unnamed x1 -> x0, local copies, waits for them, and re-layouts: 1.67 us -> none
    pallas_call x1, Pallas kernels: 32.6 us -> 31.8 us  [body(): pl.pallas_call(functools.partial(kernel, n_ctx, n_head, capacity, pieces)...]
where the time goes in v3:
time: 33.8 us; the launch traced here: 33.7 us
  Pallas kernels  33.7 us (100%)
    pallas_call x1, Pallas kernels, body(): pl.pallas_call(functools.partial(kernel, n_ctx, n_head, capacity, pieces)...  31.8 us
    pallas_call x1, Pallas kernels, body(): pl.pallas_call(place_rows, grid=(blocks,), out_shape=jax.ShapeDtypeStruct...  1.87 us

profile of v3, /device:TPU:0, one launch (start us, length us, event | category | flops | bytes accessed | tf_op | source)
XLA Modules:
  0.0 33.7 jit_solution(16375568522444205543)
XLA Ops:
  0.0 31.8 %shard_map.64 = (bf16[384,128]{1,0:T(8,128)(2,1)}, s32[1,384]{1,0:T(1,128)}) custom-call(bf16[256,128]{1,0:T(8,128)(2,1)} %ev_hbm.1, bf16[3,128,128]{2,1,0:T(8,128)(2,1)} %w_hbm.1, bf16[256,128]{1,0:T(8,128)(2,1)} %tg_hbm.1, bf16[1920,128]{1,0:T(8,128)(2,1)} %neg_hbm.1, s32[1,256]{1,0:T(1,128)} %bitcast.2, s32[1,256]{1,0:T(1,128)} %bitcast.3), custom_call_target="tpu_custom_call" | custom-call | tf_op jit(solution)/shard_map/pallas_call | solution.py:459
  31.8 1.9 %shard_map.65 = f32[512,128]{1,0:T(8,128)} custom-call(bf16[384,128]{1,0:T(8,128)(2,1)} %get-tuple-element.7.rows_ref, s32[1,384]{1,0:T(1,128)} %get-tuple-element.8.numbers_ref), custom_call_target="tpu_custom_call" | custom-call | tf_op jit(solution)/shard_map/pallas_call | solution.py:509

commit v4 on v3

--- a/solution.py
+++ b/solution.py
@@ -303,6 +303,8 @@
 
     neg_forward(0)
     inner_sum(state_mid, state_mid_in, sem_st2)
+    for r in range(1, parts):
+        neg_forward(r)
     state = acc[0:size, :]
     total = acc[size : size + 1, :]
     state_b = state.astype(BF)
@@ -339,8 +341,6 @@
     for k in range(1, n_head):
         pos_copy(k).start()
 
-    for r in range(1, parts):
-        neg_forward(r)
     for r in range(parts):
         neg_forward_cross(r)
     for k in range(1, n_head):

time: 33.8 us -> 34 us (level)
  no operation moved by 1% of the time
where the time goes in v4:
time: 34 us; the launch traced here: 33.9 us
  Pallas kernels  33.8 us (99%)
    pallas_call x1, Pallas kernels, body(): pl.pallas_call(functools.partial(kernel, n_ctx, n_head, capacity, pieces)...  32 us
    pallas_call x1, Pallas kernels, body(): pl.pallas_call(place_rows, grid=(blocks,), out_shape=jax.ShapeDtypeStruct...  1.86 us

profile of v4, /device:TPU:0, one launch (start us, length us, event | category | flops | bytes accessed | tf_op | source)
XLA Modules:
  0.0 33.9 jit_solution(12911730946508343254)
XLA Ops:
  0.0 32.0 %shard_map.64 = (bf16[384,128]{1,0:T(8,128)(2,1)}, s32[1,384]{1,0:T(1,128)}) custom-call(bf16[256,128]{1,0:T(8,128)(2,1)} %ev_hbm.1, bf16[3,128,128]{2,1,0:T(8,128)(2,1)} %w_hbm.1, bf16[256,128]{1,0:T(8,128)(2,1)} %tg_hbm.1, bf16[1920,128]{1,0:T(8,128)(2,1)} %neg_hbm.1, s32[1,256]{1,0:T(1,128)} %bitcast.2, s32[1,256]{1,0:T(1,128)} %bitcast.3), custom_call_target="tpu_custom_call" | custom-call | tf_op jit(solution)/shard_map/pallas_call | solution.py:459
  32.0 1.9 %shard_map.65 = f32[512,128]{1,0:T(8,128)} custom-call(bf16[384,128]{1,0:T(8,128)(2,1)} %get-tuple-element.7.rows_ref, s32[1,384]{1,0:T(1,128)} %get-tuple-element.8.numbers_ref), custom_call_target="tpu_custom_call" | custom-call | tf_op jit(solution)/shard_map/pallas_call | solution.py:509
